TPU v7x, 32 devices: a whole 2x2x4 slice. The times are simulated.
32 devices in a mesh: tile: 4 (over x, core), blk: 8 (over z, y).
Axes of the slice: x: 2, y: 2, z: 4, core: 2. Of those that a mesh axis runs over, the one named last changes fastest.
Arguments:
- tokens: bfloat16 [32768, 384], P(('tile', 'blk')), may hold values from -52 to 52
- ln_gain: float32 [384], replicated, may hold values from 0.1 to 1.9
- route: int32 [32768, 2], P(('tile', 'blk')), may hold values from 0 to 15, all different within a row; in each aligned block of 1024 rows (0 to 1023, 1024 to 2047, ...) at most 192 rows name the same one
- gates: float32 [32768, 2], P(('tile', 'blk')), may hold values from 0.1 to 1
- w_gate: bfloat16 [16, 384, 1024], P('tile', 'blk'), may hold values from -0.3125 to 0.3125
- w_up: bfloat16 [16, 384, 1024], P('tile', 'blk'), may hold values from -0.3125 to 0.3125
- w_down: bfloat16 [16, 1024, 384], P('tile', 'blk'), may hold values from -0.1875 to 0.1875
- d_mixed: bfloat16 [32768, 384], P(('tile', 'blk')), may hold values from -6 to 6
Outputs:
- mixed: bfloat16 [32768, 384], P(('tile', 'blk'))
- grad_gates: float32 [32768, 2], P(('tile', 'blk'))
- grad_tokens: bfloat16 [32768, 384], P(('tile', 'blk'))
- grad_w_gate: float32 [16, 384, 1024], P('tile', 'blk')
- grad_w_up: float32 [16, 384, 1024], P('tile', 'blk')
- grad_w_down: float32 [16, 1024, 384], P('tile', 'blk')
Inputs may be any that keep to these rules, and one draw needn't show every extreme that they name: `route`: each row names 2 different experts; within the rows of one device no expert is named more than 192 times, a bound that some block reaches.
All inputs are finite; a program needn't handle non-finite values.
Results may differ from a plain program's by a relative error of at most 0.014.
Values may be sent and summed in bfloat16 or wider, within the bound.
A program may use at most 192 MiB of HBM per device.

v0:
```python
import jax
import jax.numpy as jnp
from jax import lax
from jax.sharding import PartitionSpec as P


def layer_norm(values, ln_gain):
    centre = jnp.mean(values, axis=-1, keepdims=True)
    centred = values - centre
    spread = jnp.mean(centred * centred, axis=-1, keepdims=True)
    return values * lax.rsqrt(spread + 1e-05) * ln_gain


def expert_forward(inputs_rows, weight_gate, weight_up, weight_down):
    gate_pre = jnp.einsum(
        "erd,edh->erh", inputs_rows, weight_gate, preferred_element_type=jnp.float32
    )
    up_pre = jnp.einsum("erd,edh->erh", inputs_rows, weight_up, preferred_element_type=jnp.float32)
    sigma_gate = jax.nn.sigmoid(gate_pre)
    hidden_act = (gate_pre * sigma_gate * up_pre).astype(jnp.bfloat16)
    expert_rows = jnp.einsum(
        "erh,ehd->erd", hidden_act, weight_down, preferred_element_type=jnp.float32
    )
    return (expert_rows.astype(jnp.bfloat16), gate_pre, up_pre, hidden_act)


def expert_backward(
    inputs_rows, d_rows, gate_pre, up_pre, hidden_act, weight_gate, weight_up, weight_down
):
    d_act = jnp.einsum("erd,ehd->erh", d_rows, weight_down, preferred_element_type=jnp.float32)
    sigma_gate = jax.nn.sigmoid(gate_pre)
    d_gate = (d_act * up_pre * sigma_gate * (1.0 + gate_pre * (1.0 - sigma_gate))).astype(
        jnp.bfloat16
    )
    d_up = (d_act * gate_pre * sigma_gate).astype(jnp.bfloat16)
    d_in = jnp.einsum(
        "erh,edh->erd", d_gate, weight_gate, preferred_element_type=jnp.float32
    ) + jnp.einsum("erh,edh->erd", d_up, weight_up, preferred_element_type=jnp.float32)
    grad_gate = jnp.einsum("erd,erh->edh", inputs_rows, d_gate, preferred_element_type=jnp.float32)
    grad_up = jnp.einsum("erd,erh->edh", inputs_rows, d_up, preferred_element_type=jnp.float32)
    grad_down = jnp.einsum("erh,erd->ehd", hidden_act, d_rows, preferred_element_type=jnp.float32)
    return (d_in.astype(jnp.bfloat16), grad_gate, grad_up, grad_down)


def on_device(tokens, ln_gain, route, gates, w_gate, w_up, w_down, d_mixed):
    tok_rows, features = tokens.shape
    top_picks = route.shape[1]
    per_tile = w_gate.shape[0]
    tile_count = lax.axis_size("tile")
    experts_all = per_tile * tile_count
    capacity = max(2, 3 * tok_rows * top_picks // (2 * experts_all))
    tokens_wide = tokens.astype(jnp.float32)
    normed = layer_norm(tokens_wide, ln_gain).astype(jnp.bfloat16)
    flat_route = route.reshape(-1)
    onehot = (flat_route[:, None] == lax.iota(jnp.int32, experts_all)[None, :]).astype(jnp.int32)
    slot_rank = jnp.sum((jnp.cumsum(onehot, axis=0) - 1) * onehot, axis=1)
    slot_index = flat_route * capacity + slot_rank

    def pack_slots(values):
        blank = jnp.zeros((experts_all * capacity, features), jnp.bfloat16)
        return blank.at[slot_index].set(values).reshape(tile_count, per_tile, capacity, features)

    def to_experts(packed):
        arrived = lax.all_to_all(packed, "tile", split_axis=0, concat_axis=2, tiled=True)[0]
        return arrived

    def from_experts(results):
        returned = lax.all_to_all(results[None], "tile", split_axis=2, concat_axis=0, tiled=True)
        picked = returned.reshape(experts_all * capacity, features)[slot_index]
        return picked.reshape(tok_rows, top_picks, features).astype(jnp.float32)

    weight_gate, weight_up, weight_down = (
        lax.all_gather(w_gate, "blk", axis=1, tiled=True),
        lax.all_gather(w_up, "blk", axis=1, tiled=True),
        lax.all_gather(w_down, "blk", axis=1, tiled=True),
    )
    inputs_rows = to_experts(pack_slots(jnp.repeat(normed, top_picks, axis=0)))
    expert_rows, gate_pre, up_pre, hidden_act = expert_forward(
        inputs_rows, weight_gate, weight_up, weight_down
    )
    expert_out = from_experts(expert_rows)
    mixed = jnp.sum(gates[:, :, None] * expert_out, axis=1).astype(jnp.bfloat16)
    d_wide = d_mixed.astype(jnp.float32)
    grad_gates = jnp.sum(d_wide[:, None, :] * expert_out, axis=-1)
    d_out = (
        (gates[:, :, None] * d_wide[:, None, :])
        .astype(jnp.bfloat16)
        .reshape(tok_rows * top_picks, features)
    )
    d_rows = to_experts(pack_slots(d_out))
    d_in, grad_gate, grad_up, grad_down = expert_backward(
        inputs_rows, d_rows, gate_pre, up_pre, hidden_act, weight_gate, weight_up, weight_down
    )
    d_normed = jnp.sum(from_experts(d_in), axis=1)

    def normalize(values):
        return layer_norm(values, ln_gain)

    unused, pullback = jax.vjp(normalize, tokens_wide)
    grad_tokens = pullback(d_normed)[0].astype(jnp.bfloat16)
    total_gate, total_up, total_down = (
        lax.psum_scatter(
            grad_gate.astype(jnp.bfloat16), "blk", scatter_dimension=1, tiled=True
        ).astype(jnp.float32),
        lax.psum_scatter(
            grad_up.astype(jnp.bfloat16), "blk", scatter_dimension=1, tiled=True
        ).astype(jnp.float32),
        lax.psum_scatter(
            grad_down.astype(jnp.bfloat16), "blk", scatter_dimension=1, tiled=True
        ).astype(jnp.float32),
    )
    return (mixed, grad_gates, grad_tokens, total_gate, total_up, total_down)


def solution(mesh):
    placed = (
        P(("tile", "blk"), None),
        P(),
        P(("tile", "blk"), None),
        P(("tile", "blk"), None),
        P("tile", "blk", None),
        P("tile", "blk", None),
        P("tile", "blk", None),
        P(("tile", "blk"), None),
    )
    return jax.shard_map(
        on_device,
        mesh=mesh,
        in_specs=placed,
        out_specs=(
            P(("tile", "blk"), None),
            P(("tile", "blk"), None),
            P(("tile", "blk"), None),
            P("tile", "blk", None),
            P("tile", "blk", None),
            P("tile", "blk", None),
        ),
        check_vma=False,
    )
```

profile of v0, /device:TPU:0, one launch (start us, length us, event | category | flops | bytes accessed | tf_op | source)
XLA Modules:
  0.0 456.1 jit_solution(16825820951956494859)
XLA Ops:
  7.2 0.7 all-gather.4.cloned.1.call-update
  8.0 0.7 all-gather.6.cloned.1.call-update
  8.7 0.7 all-gather.8.cloned.1.call-update
  9.4 0.9 copy.34
  10.3 0.3 eq.29
  10.6 4.6 reduce-window.6
  15.2 0.4 slice_reduce_fusion
  16.1 0.5 fusion.3
  16.6 0.3 fusion.10
  16.9 0.3 eq.25
  17.4 0.3 mul.136
  17.7 0.8 broadcast_in_dim.10
  18.5 1.5 reshape.153
  20.1 11.6 %scatter_custom_fusion = bf16[3072,384]{1,0:T(8,128)(2,1)} fusion(s32[2048]{0:T(1024)S(1)} %bitcast.70, bf16[2048,384]{1,0:T(8,128)(2,1)} %reshape.153, bf16[]{:T(256)} %constant.10.clone.1), kind=kCustom, calls=%fused_computation.35 | custom fusion | bytes 2359808 | tf_op jit(solution)/shard_map/scatter | solution.py:61
  31.7 4.5 all-to-all-start
  36.2 1.0 copy.32
  37.3 1.3 mul.148
  38.6 3.6 mul.146
  42.2 5.4 %mul.150 = f32[2048,384]{1,0:T(8,128)} reshape(f32[1024,2,384]{2,1,0:T(2,128)} %mul.146) | data formatting | bytes 6291456 | tf_op jit(solution)/shard_map/mul | solution.py:84
  47.6 12.6 %scatter_custom_fusion.1 = bf16[3072,384]{1,0:T(8,128)(2,1)} fusion(s32[2048]{0:T(1024)S(1)} %bitcast.71, f32[2048,384]{1,0:T(8,128)} %mul.150, f32[2048]{0:T(1024)S(1)} %mul.148, bf16[]{:T(256)} %constant.10.clone.1), kind=kCustom, calls=%fused_computation.32 | custom fusion | flops 1572864 | bytes 5513218 | tf_op jit(solution)/shard_map/scatter | solution.py:61
  60.2 4.6 %all-to-all-done = bf16[4,4,192,384]{3,2,1,0:T(8,128)(2,1)S(1)} async-done(((bf16[4,4,192,384]{3,2,1,0:T(8,128)(2,1)}), bf16[4,4,192,384]{3,2,1,0:T(8,128)(2,1)S(1)}, u32[]{:S(2)}, u32[]{:S(2)}) %all-to-all-start) | async-done | bytes 2359328 | tf_op jit(solution)/shard_map/all_to_all | solution.py:64
  64.8 1.4 copy-done.1
  66.2 4.5 all-to-all-start.2
  70.9 1.9 copy.36
  72.9 26.3 %all-to-all-done.2 = bf16[4,4,192,384]{3,2,1,0:T(8,128)(2,1)} async-done(((bf16[4,4,192,384]{3,2,1,0:T(8,128)(2,1)}), bf16[4,4,192,384]{3,2,1,0:T(8,128)(2,1)}, u32[]{:S(2)}, u32[]{:S(2)}) %all-to-all-start.2) | async-done | bytes 2359328 | tf_op jit(solution)/shard_map/all_to_all | solution.py:64
  99.2 3.4 copy.40
  102.6 8.7 %fusion.21 = f32[4,768,1024]{2,1,0:T(8,128)} fusion(bf16[4,768,384]{2,1,0:T(8,128)(2,1)S(1)} %bitcast.58, bf16[4,384,1024]{2,1,0:T(8,128)(2,1)} %all-gather.4.cloned.1.call-done), kind=kOutput, calls=%fused_computation.53 | convolution fusion | flops 2415919104 | bytes 18087936 | tf_op jit(solution)/shard_map/erd,edh->erh/dot_general | solution.py:15
  111.3 22.6 %all-gather.6.cloned.1.call-done = bf16[4,384,1024]{2,1,0:T(8,128)(2,1)} async-done(((bf16[4,48,1024]{2,1,0:T(8,128)(2,1)}), bf16[4,384,1024]{2,1,0:T(8,128)(2,1)}) %all-gather.6.cloned.1.call-update) | async-done | bytes 3145744 | tf_op jit(solution)/shard_map/all_gather | solution.py:74
  133.9 8.3 %fusion.22 = f32[4,768,1024]{2,1,0:T(8,128)} fusion(bf16[4,768,384]{2,1,0:T(8,128)(2,1)S(1)} %bitcast.59, bf16[4,384,1024]{2,1,0:T(8,128)(2,1)} %all-gather.6.cloned.1.call-done), kind=kOutput, calls=%fused_computation.54 | convolution fusion | flops 2415919104 | bytes 18087936 | tf_op jit(solution)/shard_map/erd,edh->erh/dot_general | solution.py:18
  142.2 52.6 %all-gather.8.cloned.1.call-done = bf16[4,1024,384]{2,1,0:T(8,128)(2,1)} async-done(((bf16[4,128,384]{2,1,0:T(8,128)(2,1)}), bf16[4,1024,384]{2,1,0:T(8,128)(2,1)}) %all-gather.8.cloned.1.call-update) | async-done | bytes 3145744 | tf_op jit(solution)/shard_map/all_gather | solution.py:75
  194.8 18.0 %multiply_convert_fusion = (bf16[4,768,1024]{2,1,0:T(8,128)(2,1)}, bf16[4,768,1024]{2,1,0:T(8,128)(2,1)}, bf16[4,768,1024]{2,1,0:T(8,128)(2,1)}) fusion(f32[4,768,1024]{2,1,0:T(8,128)} %fusion.21, f32[4,768,1024]{2,1,0:T(8,128)} %fusion.22, bf16[4,768,384]{2,1,0:T(8,128)(2,1)} %bitcast.66, bf16[4,1024,384]{2,1,0:T(8,128)(2,1)} %all-gather.8.cloned.1.call-done), kind=kOutput, calls=%fused_computation.4 | convolution fusion | flops 2466250752 | bytes 49545216 | tf_op jit(solution)/shard_map/erd,ehd->erh/dot_general | solution.py:30
  212.8 7.1 %convolution_convert_fusion.2 = bf16[4,384,1024]{2,1,0:T(8,128)(2,1)} fusion(bf16[4,768,384]{2,1,0:T(8,128)(2,1)S(1)} %bitcast.60, bf16[4,768,1024]{2,1,0:T(8,128)(2,1)} %get-tuple-element.15), kind=kOutput, calls=%fused_computation.20 | convolution fusion | flops 2417491968 | bytes 11796480 | tf_op jit(solution)/shard_map/erd,erh->edh/dot_general | solution.py:39
  219.9 0.5 reduce-scatter.6.cloned.1.call-start
  220.5 7.1 %convolution_convert_fusion.1 = bf16[4,384,1024]{2,1,0:T(8,128)(2,1)} fusion(bf16[4,768,384]{2,1,0:T(8,128)(2,1)S(1)} %bitcast.61, bf16[4,768,1024]{2,1,0:T(8,128)(2,1)} %get-tuple-element.14), kind=kOutput, calls=%fused_computation.19 | convolution fusion | flops 2417491968 | bytes 11796480 | tf_op jit(solution)/shard_map/erd,erh->edh/dot_general | solution.py:40
  227.7 1.6 copy-done.7
  229.3 8.0 %convolution_convert_fusion = bf16[4,1024,384]{2,1,0:T(8,128)(2,1)} fusion(bf16[4,768,1024]{2,1,0:T(8,128)(2,1)} %get-tuple-element.16, bf16[4,768,384]{2,1,0:T(8,128)(2,1)S(1)} %bitcast.67), kind=kOutput, calls=%fused_computation.18 | convolution fusion | flops 2417491968 | bytes 11796480 | tf_op jit(solution)/shard_map/erh,erd->ehd/dot_general | solution.py:41
  237.3 6.7 %fusion.23 = f32[4,768,384]{2,1,0:T(8,128)S(1)} fusion(bf16[4,768,1024]{2,1,0:T(8,128)(2,1)} %get-tuple-element.15, bf16[4,384,1024]{2,1,0:T(8,128)(2,1)} %all-gather.4.cloned.1.call-done), kind=kOutput, calls=%fused_computation.55 | convolution fusion | flops 2415919104 | bytes 14155776 | tf_op jit(solution)/shard_map/erh,edh->erd/dot_general | solution.py:36
  244.1 3.7 fusion
  247.8 3.2 copy.41
  251.0 3.6 all-to-all-start.3
  254.7 7.2 %convert_bitcast_fusion = bf16[1,4,768,384]{3,2,1,0:T(8,128)(2,1)S(1)} fusion(bf16[4,768,1024]{2,1,0:T(8,128)(2,1)} %get-tuple-element.16, bf16[4,1024,384]{2,1,0:T(8,128)(2,1)} %all-gather.8.cloned.1.call-done), kind=kOutput, calls=%fused_computation.17 | convolution fusion | flops 2417098752 | bytes 11796480 | tf_op jit(solution)/shard_map/erh,ehd->erd/dot_general | solution.py:21
  261.9 3.3 copy.37
  265.1 18.0 %all-to-all-done.3 = bf16[1,4,768,384]{3,1,0,2:T(4,128)(2,1)S(1)} async-done(((bf16[1,4,768,384]{3,1,0,2:T(4,128)(2,1)}), bf16[1,4,768,384]{3,1,0,2:T(4,128)(2,1)S(1)}, u32[]{:S(2)}, u32[]{:S(2)}) %all-to-all-start.3) | async-done | bytes 2359328 | tf_op jit(solution)/shard_map/all_to_all | solution.py:68
  283.1 1.4 copy-done.2
  284.5 4.7 %all-to-all-start.1 = ((bf16[1,4,768,384]{3,1,0,2:T(4,128)(2,1)}), bf16[1,4,768,384]{3,1,0,2:T(4,128)(2,1)}, u32[]{:S(2)}, u32[]{:S(2)}) async-start(bf16[1,4,768,384]{3,1,0,2:T(4,128)(2,1)} %copy.37), calls=%async_computation.1 | async-start | bytes 4718592 | tf_op jit(solution)/shard_map/all_to_all | solution.py:68
  289.2 2.6 convert_element_type.81
  291.8 0.4 copy.42
  292.2 9.0 %gather_fusion.1 = bf16[2048,384]{1,0:T(8,128)(2,1)} fusion(bf16[3072,384]{1,0:T(8,128)(2,1)S(1)} %bitcast.57, s32[2048]{0:T(1024)S(1)} %broadcast_clamp_fusion), kind=kCustom, calls=%fused_computation.1 | custom fusion | bytes 3153920 | tf_op jit(solution)/shard_map/gather | solution.py:69
  301.2 4.9 %reshape.132 = f32[1024,2,384]{2,1,0:T(2,128)} reshape(bf16[2048,384]{1,0:T(8,128)(2,1)} %gather_fusion.1) | data formatting | bytes 4718592 | tf_op jit(solution)/shard_map/convert_element_type | solution.py:70
  306.1 11.6 %all-to-all-done.1 = bf16[1,4,768,384]{3,1,0,2:T(4,128)(2,1)} async-done(((bf16[1,4,768,384]{3,1,0,2:T(4,128)(2,1)}), bf16[1,4,768,384]{3,1,0,2:T(4,128)(2,1)}, u32[]{:S(2)}, u32[]{:S(2)}) %all-to-all-start.1) | async-done | bytes 2359328 | tf_op jit(solution)/shard_map/all_to_all | solution.py:68
  317.7 2.1 copy.38
  319.9 9.1 %gather_fusion = bf16[2048,384]{1,0:T(8,128)(2,1)} fusion(bf16[3072,384]{1,0:T(8,128)(2,1)S(1)} %bitcast.56, s32[2048]{0:T(1024)S(1)} %broadcast_clamp_fusion), kind=kCustom, calls=%fused_computation | custom fusion | bytes 3153920 | tf_op jit(solution)/shard_map/gather | solution.py:69
  328.9 5.0 %reshape.131 = f32[1024,2,384]{2,1,0:T(2,128)} reshape(bf16[2048,384]{1,0:T(8,128)(2,1)} %gather_fusion) | data formatting | bytes 4718592 | tf_op jit(solution)/shard_map/convert_element_type | solution.py:70
  334.0 10.1 %multiply_reduce_fusion = (f32[1024,2]{1,0:T(8,128)S(1)}, bf16[1024,384]{1,0:T(8,128)(2,1)}) fusion(f32[1024,2,384]{2,1,0:T(2,128)} %reshape.131, f32[1024,384]{1,0:T(8,128)S(1)} %copy-done.4, f32[1024,2]{1,0:T(8,128)S(1)} %copy-done.5), kind=kLoop, calls=%fused_computation.10 | loop fusion | flops 2750464 | bytes 5521408 | tf_op jit(solution)/shard_map/reduce_sum | solution.py:84
  344.1 0.8 copy.46
  344.9 5.7 %reduce_sum.96 = f32[1024,384]{1,0:T(8,128)S(1)} reduce(f32[1024,2,384]{2,1,0:T(2,128)} %reshape.132, f32[]{:T(128)} %constant.25.clone.1), dimensions={1}, to_apply=%region_9.10 | reduce | flops 393216 | bytes 4718596 | tf_op jit(solution)/shard_map/reduce_sum | solution.py:94
  350.5 0.3 fusion.11
  350.8 0.5 fusion.5
  351.3 1.7 fusion.8
  353.0 2.0 convert_element_type.90
  355.0 15.0 %reduce-scatter.6.cloned.1.call-done = bf16[4,48,1024]{2,1,0:T(8,128)(2,1)} async-done(((bf16[4,384,1024]{2,1,0:T(8,128)(2,1)}), bf16[4,48,1024]{2,1,0:T(8,128)(2,1)}) %reduce-scatter.6.cloned.1.call-update) | async-done | bytes 393232 | tf_op jit(solution)/shard_map/reduce_scatter | solution.py:105
  370.0 2.0 convert_element_type.92
  372.0 75.1 %reduce-scatter.8.cloned.1.call-done = bf16[4,128,384]{2,1,0:T(8,128)(2,1)} async-done(((bf16[4,1024,384]{2,1,0:T(8,128)(2,1)}), bf16[4,128,384]{2,1,0:T(8,128)(2,1)}) %reduce-scatter.8.cloned.1.call-update) | async-done | bytes 393232 | tf_op jit(solution)/shard_map/reduce_scatter | solution.py:108
  447.1 1.9 convert_element_type.94
  (47 shorter events, 1.5 us)
Async XLA Ops:
  7.2 8.7 %copy-start = (bf16[1024,384]{1,0:T(8,128)(2,1)S(1)}, bf16[1024,384]{1,0:T(8,128)(2,1)}, u32[]{:S(2)}) copy-start(bf16[1024,384]{1,0:T(8,128)(2,1)} %param.8) | copy-start | bytes 2359300
  7.2 9.4 %copy-start.9 = (f32[384]{0:T(512)S(1)}, f32[384]{0:T(512)}, u32[]{:S(2)}) copy-start(f32[384]{0:T(512)} %param.9) | copy-start | bytes 4612
  7.2 95.4 %all-gather.4.cloned.1.call-start = ((), (), s32[]{:S(2)}) async-start(), calls=%async_computation.7 | async-start | bytes 3538944 | tf_op jit(solution)/shard_map/all_gather | solution.py:73
  7.9 126.0 %all-gather.6.cloned.1.call-start = ((), (), s32[]{:S(2)}) async-start(), calls=%async_computation.8 | async-start | bytes 3538944 | tf_op jit(solution)/shard_map/all_gather | solution.py:74
  8.7 186.1 %all-gather.8.cloned.1.call-start = ((), (), s32[]{:S(2)}) async-start(), calls=%async_computation.9 | async-start | bytes 3538944 | tf_op jit(solution)/shard_map/all_gather | solution.py:75
  10.3 6.5 %copy-start.8 = (s32[1024,2]{0,1:T(2,128)S(1)}, s32[1024,2]{0,1:T(2,128)}, u32[]{:S(2)}) copy-start(s32[1024,2]{0,1:T(2,128)} %param.10) | copy-start | bytes 24580
  31.7 4.5 copy-start.10
  31.7 33.1 %all-to-all-start = ((bf16[4,4,192,384]{3,2,1,0:T(8,128)(2,1)}), bf16[4,4,192,384]{3,2,1,0:T(8,128)(2,1)S(1)}, u32[]{:S(2)}, u32[]{:S(2)}) async-start(bf16[4,4,192,384]{3,2,1,0:T(8,128)(2,1)} %bitcast.65), calls=%async_computation | async-start | bytes 4718592 | tf_op jit(solution)/shard_map/all_to_all | solution.py:64
  64.8 1.4 copy-start.1
  66.2 33.0 %all-to-all-start.2 = ((bf16[4,4,192,384]{3,2,1,0:T(8,128)(2,1)}), bf16[4,4,192,384]{3,2,1,0:T(8,128)(2,1)}, u32[]{:S(2)}, u32[]{:S(2)}) async-start(bf16[4,4,192,384]{3,2,1,0:T(8,128)(2,1)} %bitcast.64), calls=%async_computation.2 | async-start | bytes 4718592 | tf_op jit(solution)/shard_map/all_to_all | solution.py:64
  70.7 282.4 %reduce-scatter.4.cloned.1.call-start = ((), (), s32[]{:S(2)}) async-start(), calls=%async_computation.10 | async-start | bytes 3538944 | tf_op jit(solution)/shard_map/reduce_scatter | solution.py:102
  219.9 150.1 %reduce-scatter.6.cloned.1.call-start = ((), (), s32[]{:S(2)}) async-start(), calls=%async_computation.11 | async-start | bytes 3538944 | tf_op jit(solution)/shard_map/reduce_scatter | solution.py:105
  227.6 1.7 copy-start.7
  227.6 219.5 %reduce-scatter.8.cloned.1.call-start = ((), (), s32[]{:S(2)}) async-start(), calls=%async_computation.12 | async-start | bytes 3538944 | tf_op jit(solution)/shard_map/reduce_scatter | solution.py:108
  237.2 6.7 %slice-start = ((s8[6291456]{0:T(1024)(128)(4,1)}), s8[2097152]{0:T(1024)(128)(4,1)S(1)}, s32[]{:S(2)}) async-start(s8[6291456]{0:T(1024)(128)(4,1)} %bitcast.74), calls=%async_computation.13 | async-start | bytes 4194304
  237.2 6.7 %copy-start.6 = (bf16[4,384,1024]{2,1,0:T(8,128)(2,1)S(1)}, bf16[4,384,1024]{2,1,0:T(8,128)(2,1)}, u32[]{:S(2)}) copy-start(bf16[4,384,1024]{2,1,0:T(8,128)(2,1)} %all-gather.6.cloned.1.call-done) | copy-start | bytes 9437188
  237.2 6.8 %slice-start.1 = ((s8[6291456]{0:T(1024)(128)(4,1)}), s8[4194304]{0:T(1024)(128)(4,1)S(1)}, s32[]{:S(2)}) async-start(s8[6291456]{0:T(1024)(128)(4,1)} %bitcast.74), calls=%async_computation.14 | async-start | bytes 8388608
  251.0 32.1 %all-to-all-start.3 = ((bf16[1,4,768,384]{3,1,0,2:T(4,128)(2,1)}), bf16[1,4,768,384]{3,1,0,2:T(4,128)(2,1)S(1)}, u32[]{:S(2)}, u32[]{:S(2)}) async-start(bf16[1,4,768,384]{3,1,0,2:T(4,128)(2,1)} %copy.41), calls=%async_computation.3 | async-start | bytes 4718592 | tf_op jit(solution)/shard_map/all_to_all | solution.py:68
  283.1 1.4 copy-start.2
  284.5 33.2 %all-to-all-start.1 = ((bf16[1,4,768,384]{3,1,0,2:T(4,128)(2,1)}), bf16[1,4,768,384]{3,1,0,2:T(4,128)(2,1)}, u32[]{:S(2)}, u32[]{:S(2)}) async-start(bf16[1,4,768,384]{3,1,0,2:T(4,128)(2,1)} %copy.37), calls=%async_computation.1 | async-start | bytes 4718592 | tf_op jit(solution)/shard_map/all_to_all | solution.py:68
  289.2 2.6 copy-start.3
  328.9 5.0 %copy-start.4 = (f32[1024,384]{1,0:T(8,128)S(1)}, f32[1024,384]{1,0:T(8,128)}, u32[]{:S(2)}) copy-start(f32[1024,384]{1,0:T(8,128)} %convert_element_type.81) | copy-start | bytes 4718596
  328.9 5.0 %copy-start.5 = (f32[1024,2]{1,0:T(8,128)S(1)}, f32[1024,2]{1,0:T(8,128)}, u32[]{:S(2)}) copy-start(f32[1024,2]{1,0:T(8,128)} %copy.32) | copy-start | bytes 24580
Sparse Core Ops, SparseCore 0:
  10.2 62.7 all-gather.3
  75.2 58.6 all-gather.5
  136.1 58.6 all-gather.7
  220.1 72.9 reduce-scatter.3
  296.5 73.4 reduce-scatter.5
  373.4 73.5 reduce-scatter.7
where the time goes:
time: 463 us; the launch traced here: 456 us
  waiting for transfers between devices  228 us (49%)
  local copies, waits for them, and re-layouts  75.3 us (16%)
  matrix products  74.9 us (16%)
  other arithmetic  45.1 us (10%)
  starting transfers between devices  18.2 us (4%)
  between operations  14.6 us (3%)
    reduce_scatter x1, waiting for transfers between devices, on_device(): lax.psum_scatter(grad_down.astype(jnp.bfloat16), 'blk', scatter_dimension...  75.1 us
    all_gather x1, waiting for transfers between devices, on_device(): lax.all_gather(w_down, 'blk', axis=1, tiled=True)  52.6 us
    all_to_all x2, waiting for transfers between devices, to_experts(): lax.all_to_all(packed, 'tile', split_axis=0, concat_axis=2, tiled=True)[0]  30.9 us
    all_to_all x2, waiting for transfers between devices, from_experts(): lax.all_to_all(results[None], 'tile', split_axis=2, concat_axis=0, tiled=...  29.6 us
    all_gather x1, waiting for transfers between devices, on_device(): lax.all_gather(w_up, 'blk', axis=1, tiled=True)  22.6 us
    gather x2, local copies, waits for them, and re-layouts, from_experts(): picked = returned.reshape(experts_all * capacity, features)[slot_index]  18.1 us
    dot_general x1, matrix products, expert_backward(): jnp.einsum('erd,ehd->erh', d_rows, weight_down, preferred_element_type=jn...  18 us
    reduce_scatter x1, waiting for transfers between devices, on_device(): lax.psum_scatter(grad_up.astype(jnp.bfloat16), 'blk', scatter_dimension=1...  15 us
  transfers between devices with their start and end apart: 10, of which 8 were waited for; matrix products, arithmetic and copies ran while one was open for 36% of the time, Pallas kernels for 0%

commit v1 on v0

--- a/solution.py
+++ b/solution.py
@@ -72,7 +72,7 @@
     weight_gate, weight_up, weight_down = (
         lax.all_gather(w_gate, "blk", axis=1, tiled=True),
         lax.all_gather(w_up, "blk", axis=1, tiled=True),
-        lax.all_gather(w_down, "blk", axis=1, tiled=True),
+        jnp.concatenate(lax.all_gather(w_down, "blk"), axis=1),
     )
     inputs_rows = to_experts(pack_slots(jnp.repeat(normed, top_picks, axis=0)))
     expert_rows, gate_pre, up_pre, hidden_act = expert_forward(

time: 463 us -> 472 us (1.019)
  waiting for transfers between devices: 228 us -> 233 us
    all_gather x1, waiting for transfers between devices: 52.6 us -> 0.01 us  [on_device(): lax.all_gather(w_down, 'blk')]
    all_gather x1, waiting for transfers between devices: 22.6 us -> 52.5 us  [on_device(): lax.all_gather(w_up, 'blk', axis=1, tiled=True)]
    all_gather x1, waiting for transfers between devices: 0.01 us -> 26.9 us  [on_device(): lax.all_gather(w_gate, 'blk', axis=1, tiled=True)]
  transfers between devices with their start and end apart: 10 -> 10, of which waited for: 8 -> 8; matrix products, arithmetic and copies ran while one was open for 36% -> 34% of each run, Pallas kernels for 0% -> 0%
where the time goes in v1:
time: 472 us; the launch traced here: 465 us
  waiting for transfers between devices  233 us (49%)
  local copies, waits for them, and re-layouts  79.7 us (17%)
  matrix products  74.5 us (16%)
  other arithmetic  45.1 us (10%)
  starting transfers between devices  18.2 us (4%)
  between operations  14.6 us (3%)
    reduce_scatter x1, waiting for transfers between devices, on_device(): lax.psum_scatter(grad_down.astype(jnp.bfloat16), 'blk', scatter_dimension...  75.4 us
    all_gather x1, waiting for transfers between devices, on_device(): lax.all_gather(w_up, 'blk', axis=1, tiled=True)  52.5 us
    all_to_all x2, waiting for transfers between devices, to_experts(): lax.all_to_all(packed, 'tile', split_axis=0, concat_axis=2, tiled=True)[0]  30.9 us
    all_to_all x2, waiting for transfers between devices, from_experts(): lax.all_to_all(results[None], 'tile', split_axis=2, concat_axis=0, tiled=...  29.6 us
    all_gather x1, waiting for transfers between devices, on_device(): lax.all_gather(w_gate, 'blk', axis=1, tiled=True)  26.9 us
    gather x2, local copies, waits for them, and re-layouts, from_experts(): picked = returned.reshape(experts_all * capacity, features)[slot_index]  18.1 us
    dot_general x1, matrix products, expert_backward(): jnp.einsum('erd,ehd->erh', d_rows, weight_down, preferred_element_type=jn...  18 us
    reduce_scatter x1, waiting for transfers between devices, on_device(): lax.psum_scatter(grad_up.astype(jnp.bfloat16), 'blk', scatter_dimension=1...  15.3 us
  transfers between devices with their start and end apart: 10, of which 8 were waited for; matrix products, arithmetic and copies ran while one was open for 34% of the time, Pallas kernels for 0%

profile of v1, /device:TPU:0, one launch (start us, length us, event | category | flops | bytes accessed | tf_op | source)
XLA Modules:
  0.0 464.9 jit_solution(13942725846949269249)
XLA Ops:
  7.2 0.7 all-gather.9.cloned.1.call-update
  8.0 0.7 all-gather.5.cloned.1.call-update
  8.7 0.7 all-gather.7.cloned.1.call-update
  9.4 0.9 copy.36
  10.3 0.3 eq.29
  10.6 0.3 eq.25
  10.9 4.6 reduce-window.6
  15.5 0.4 slice_reduce_fusion
  16.3 0.3 mul.136
  16.9 0.5 fusion.3
  17.6 0.8 broadcast_in_dim.10
  18.4 1.5 reshape.161
  20.1 11.5 %scatter_custom_fusion = bf16[3072,384]{1,0:T(8,128)(2,1)} fusion(s32[2048]{0:T(1024)S(1)} %bitcast.77, bf16[2048,384]{1,0:T(8,128)(2,1)} %reshape.161, bf16[]{:T(256)} %constant.10.clone.1), kind=kCustom, calls=%fused_computation.35 | custom fusion | bytes 2359808 | tf_op jit(solution)/shard_map/scatter | solution.py:61
  31.7 4.5 all-to-all-start
  36.2 1.0 copy.34
  37.2 1.3 mul.148
  38.5 3.6 mul.146
  42.2 5.4 %mul.150 = f32[2048,384]{1,0:T(8,128)} reshape(f32[1024,2,384]{2,1,0:T(2,128)} %mul.146) | data formatting | bytes 6291456 | tf_op jit(solution)/shard_map/mul | solution.py:84
  47.6 12.5 %scatter_custom_fusion.1 = bf16[3072,384]{1,0:T(8,128)(2,1)} fusion(s32[2048]{0:T(1024)S(1)} %bitcast.78, f32[2048,384]{1,0:T(8,128)} %mul.150, f32[2048]{0:T(1024)S(1)} %mul.148, bf16[]{:T(256)} %constant.10.clone.1), kind=kCustom, calls=%fused_computation.32 | custom fusion | flops 1572864 | bytes 5513218 | tf_op jit(solution)/shard_map/scatter | solution.py:61
  60.1 4.6 all-to-all-done
  64.7 1.5 copy-done.1
  66.2 4.5 all-to-all-start.2
  71.0 1.9 copy.38
  72.9 26.3 %all-to-all-done.2 = bf16[4,4,192,384]{3,2,1,0:T(8,128)(2,1)} async-done(((bf16[4,4,192,384]{3,2,1,0:T(8,128)(2,1)}), bf16[4,4,192,384]{3,2,1,0:T(8,128)(2,1)}, u32[]{:S(2)}, u32[]{:S(2)}) %all-to-all-start.2) | async-done | bytes 2359328 | tf_op jit(solution)/shard_map/all_to_all | solution.py:64
  99.2 3.4 copy.43
  102.6 4.4 copy.39
  107.0 26.9 %all-gather.5.cloned.1.call-done = bf16[4,384,1024]{2,1,0:T(8,128)(2,1)} async-done(((bf16[4,48,1024]{2,1,0:T(8,128)(2,1)}), bf16[4,384,1024]{2,1,0:T(8,128)(2,1)}) %all-gather.5.cloned.1.call-update) | async-done | bytes 3145744 | tf_op jit(solution)/shard_map/all_gather | solution.py:73
  133.9 8.4 %fusion.21 = f32[4,768,1024]{2,1,0:T(8,128)} fusion(bf16[4,768,384]{2,1,0:T(8,128)(2,1)S(1)} %bitcast.62, bf16[4,384,1024]{2,1,0:T(8,128)(2,1)} %all-gather.5.cloned.1.call-done), kind=kOutput, calls=%fused_computation.53 | convolution fusion | flops 2415919104 | bytes 18087936 | tf_op jit(solution)/shard_map/erd,edh->erh/dot_general | solution.py:15
  142.3 52.5 %all-gather.7.cloned.1.call-done = bf16[4,384,1024]{2,1,0:T(8,128)(2,1)} async-done(((bf16[4,48,1024]{2,1,0:T(8,128)(2,1)}), bf16[4,384,1024]{2,1,0:T(8,128)(2,1)}) %all-gather.7.cloned.1.call-update) | async-done | bytes 3145744 | tf_op jit(solution)/shard_map/all_gather | solution.py:74
  194.8 8.2 %fusion.22 = f32[4,768,1024]{2,1,0:T(8,128)} fusion(bf16[4,768,384]{2,1,0:T(8,128)(2,1)S(1)} %bitcast.63, bf16[4,384,1024]{2,1,0:T(8,128)(2,1)} %all-gather.7.cloned.1.call-done), kind=kOutput, calls=%fused_computation.54 | convolution fusion | flops 2415919104 | bytes 18087936 | tf_op jit(solution)/shard_map/erd,edh->erh/dot_general | solution.py:18
  203.0 18.0 %multiply_convert_fusion = (bf16[4,768,1024]{2,1,0:T(8,128)(2,1)}, bf16[4,768,1024]{2,1,0:T(8,128)(2,1)}, bf16[4,768,1024]{2,1,0:T(8,128)(2,1)}) fusion(f32[4,768,1024]{2,1,0:T(8,128)} %fusion.21, f32[4,768,1024]{2,1,0:T(8,128)} %fusion.22, bf16[4,768,384]{2,1,0:T(8,128)(2,1)} %bitcast.73, bf16[4,1024,384]{2,1,0:T(8,128)(2,1)} %bitcast.71), kind=kOutput, calls=%fused_computation.4 | convolution fusion | flops 2466250752 | bytes 49545216 | tf_op jit(solution)/shard_map/erd,ehd->erh/dot_general | solution.py:30
  221.1 7.1 %convolution_convert_fusion.2 = bf16[4,384,1024]{2,1,0:T(8,128)(2,1)} fusion(bf16[4,768,384]{2,1,0:T(8,128)(2,1)S(1)} %bitcast.64, bf16[4,768,1024]{2,1,0:T(8,128)(2,1)} %get-tuple-element.15), kind=kOutput, calls=%fused_computation.20 | convolution fusion | flops 2417491968 | bytes 11796480 | tf_op jit(solution)/shard_map/erd,erh->edh/dot_general | solution.py:39
  228.2 0.5 reduce-scatter.6.cloned.1.call-start
  228.7 7.1 %convolution_convert_fusion.1 = bf16[4,384,1024]{2,1,0:T(8,128)(2,1)} fusion(bf16[4,768,384]{2,1,0:T(8,128)(2,1)S(1)} %bitcast.65, bf16[4,768,1024]{2,1,0:T(8,128)(2,1)} %get-tuple-element.14), kind=kOutput, calls=%fused_computation.19 | convolution fusion | flops 2417491968 | bytes 11796480 | tf_op jit(solution)/shard_map/erd,erh->edh/dot_general | solution.py:40
  235.9 1.6 copy-done.7
  237.5 8.0 %convolution_convert_fusion = bf16[4,1024,384]{2,1,0:T(8,128)(2,1)} fusion(bf16[4,768,1024]{2,1,0:T(8,128)(2,1)} %get-tuple-element.16, bf16[4,768,384]{2,1,0:T(8,128)(2,1)S(1)} %bitcast.74), kind=kOutput, calls=%fused_computation.18 | convolution fusion | flops 2417491968 | bytes 11796480 | tf_op jit(solution)/shard_map/erh,erd->ehd/dot_general | solution.py:41
  245.5 6.7 %fusion.23 = f32[4,768,384]{2,1,0:T(8,128)S(1)} fusion(bf16[4,768,1024]{2,1,0:T(8,128)(2,1)} %get-tuple-element.15, bf16[4,384,1024]{2,1,0:T(8,128)(2,1)} %all-gather.5.cloned.1.call-done), kind=kOutput, calls=%fused_computation.55 | convolution fusion | flops 2415919104 | bytes 14155776 | tf_op jit(solution)/shard_map/erh,edh->erd/dot_general | solution.py:36
  252.3 3.7 fusion
  256.1 3.2 copy.44
  259.3 3.6 all-to-all-start.3
  262.9 7.2 %convert_bitcast_fusion = bf16[1,4,768,384]{3,2,1,0:T(8,128)(2,1)S(1)} fusion(bf16[4,768,1024]{2,1,0:T(8,128)(2,1)} %get-tuple-element.16, bf16[4,1024,384]{2,1,0:T(8,128)(2,1)} %bitcast.72), kind=kOutput, calls=%fused_computation.17 | convolution fusion | flops 2417098752 | bytes 11796480 | tf_op jit(solution)/shard_map/erh,ehd->erd/dot_general | solution.py:21
  270.2 3.3 copy.40
  273.4 18.0 %all-to-all-done.3 = bf16[1,4,768,384]{3,1,0,2:T(4,128)(2,1)S(1)} async-done(((bf16[1,4,768,384]{3,1,0,2:T(4,128)(2,1)}), bf16[1,4,768,384]{3,1,0,2:T(4,128)(2,1)S(1)}, u32[]{:S(2)}, u32[]{:S(2)}) %all-to-all-start.3) | async-done | bytes 2359328 | tf_op jit(solution)/shard_map/all_to_all | solution.py:68
  291.4 1.4 copy-done.2
  292.8 4.7 %all-to-all-start.1 = ((bf16[1,4,768,384]{3,1,0,2:T(4,128)(2,1)}), bf16[1,4,768,384]{3,1,0,2:T(4,128)(2,1)}, u32[]{:S(2)}, u32[]{:S(2)}) async-start(bf16[1,4,768,384]{3,1,0,2:T(4,128)(2,1)} %copy.40), calls=%async_computation.1 | async-start | bytes 4718592 | tf_op jit(solution)/shard_map/all_to_all | solution.py:68
  297.5 2.6 convert_element_type.81
  300.0 0.4 copy.45
  300.4 9.0 %gather_fusion.1 = bf16[2048,384]{1,0:T(8,128)(2,1)} fusion(bf16[3072,384]{1,0:T(8,128)(2,1)S(1)} %bitcast.61, s32[2048]{0:T(1024)S(1)} %broadcast_clamp_fusion), kind=kCustom, calls=%fused_computation.1 | custom fusion | bytes 3153920 | tf_op jit(solution)/shard_map/gather | solution.py:69
  309.5 4.9 %reshape.140 = f32[1024,2,384]{2,1,0:T(2,128)} reshape(bf16[2048,384]{1,0:T(8,128)(2,1)} %gather_fusion.1) | data formatting | bytes 4718592 | tf_op jit(solution)/shard_map/convert_element_type | solution.py:70
  314.4 11.6 %all-to-all-done.1 = bf16[1,4,768,384]{3,1,0,2:T(4,128)(2,1)} async-done(((bf16[1,4,768,384]{3,1,0,2:T(4,128)(2,1)}), bf16[1,4,768,384]{3,1,0,2:T(4,128)(2,1)}, u32[]{:S(2)}, u32[]{:S(2)}) %all-to-all-start.1) | async-done | bytes 2359328 | tf_op jit(solution)/shard_map/all_to_all | solution.py:68
  326.0 2.1 copy.41
  328.1 9.1 %gather_fusion = bf16[2048,384]{1,0:T(8,128)(2,1)} fusion(bf16[3072,384]{1,0:T(8,128)(2,1)S(1)} %bitcast.60, s32[2048]{0:T(1024)S(1)} %broadcast_clamp_fusion), kind=kCustom, calls=%fused_computation | custom fusion | bytes 3153920 | tf_op jit(solution)/shard_map/gather | solution.py:69
  337.2 5.0 %reshape.139 = f32[1024,2,384]{2,1,0:T(2,128)} reshape(bf16[2048,384]{1,0:T(8,128)(2,1)} %gather_fusion) | data formatting | bytes 4718592 | tf_op jit(solution)/shard_map/convert_element_type | solution.py:70
  342.2 10.1 %multiply_reduce_fusion = (f32[1024,2]{1,0:T(8,128)S(1)}, bf16[1024,384]{1,0:T(8,128)(2,1)}) fusion(f32[1024,2,384]{2,1,0:T(2,128)} %reshape.139, f32[1024,384]{1,0:T(8,128)S(1)} %copy-done.4, f32[1024,2]{1,0:T(8,128)S(1)} %copy-done.5), kind=kLoop, calls=%fused_computation.10 | loop fusion | flops 2750464 | bytes 5521408 | tf_op jit(solution)/shard_map/reduce_sum | solution.py:84
  352.3 0.8 copy.49
  353.1 5.7 %reduce_sum.96 = f32[1024,384]{1,0:T(8,128)S(1)} reduce(f32[1024,2,384]{2,1,0:T(2,128)} %reshape.140, f32[]{:T(128)} %constant.25.clone.1), dimensions={1}, to_apply=%region_9.10 | reduce | flops 393216 | bytes 4718596 | tf_op jit(solution)/shard_map/reduce_sum | solution.py:94
  358.8 0.3 fusion.11
  359.0 0.5 fusion.5
  359.6 1.7 fusion.8
  361.3 2.0 convert_element_type.90
  363.3 15.3 %reduce-scatter.6.cloned.1.call-done = bf16[4,48,1024]{2,1,0:T(8,128)(2,1)} async-done(((bf16[4,384,1024]{2,1,0:T(8,128)(2,1)}), bf16[4,48,1024]{2,1,0:T(8,128)(2,1)}) %reduce-scatter.6.cloned.1.call-update) | async-done | bytes 393232 | tf_op jit(solution)/shard_map/reduce_scatter | solution.py:105
  378.6 2.0 convert_element_type.92
  380.5 75.4 %reduce-scatter.8.cloned.1.call-done = bf16[4,128,384]{2,1,0:T(8,128)(2,1)} async-done(((bf16[4,1024,384]{2,1,0:T(8,128)(2,1)}), bf16[4,128,384]{2,1,0:T(8,128)(2,1)}) %reduce-scatter.8.cloned.1.call-update) | async-done | bytes 393232 | tf_op jit(solution)/shard_map/reduce_scatter | solution.py:108
  455.9 1.9 convert_element_type.94
  (48 shorter events, 1.7 us)
Async XLA Ops:
  7.2 3.7 copy-start.8
  7.2 9.5 %copy-start = (bf16[1024,384]{1,0:T(8,128)(2,1)S(1)}, bf16[1024,384]{1,0:T(8,128)(2,1)}, u32[]{:S(2)}) copy-start(bf16[1024,384]{1,0:T(8,128)(2,1)} %param.8) | copy-start | bytes 2359300
  7.2 95.4 %all-gather.9.cloned.1.call-start = ((), (), s32[]{:S(2)}) async-start(), calls=%async_computation.12 | async-start | bytes 3538944 | tf_op jit(solution)/shard_map/all_gather | solution.py:75
  7.9 126.0 %all-gather.5.cloned.1.call-start = ((), (), s32[]{:S(2)}) async-start(), calls=%async_computation.7 | async-start | bytes 3538944 | tf_op jit(solution)/shard_map/all_gather | solution.py:73
  8.7 186.1 %all-gather.7.cloned.1.call-start = ((), (), s32[]{:S(2)}) async-start(), calls=%async_computation.8 | async-start | bytes 3538944 | tf_op jit(solution)/shard_map/all_gather | solution.py:74
  9.4 7.9 %copy-start.9 = (f32[384]{0:T(512)S(1)}, f32[384]{0:T(512)}, u32[]{:S(2)}) copy-start(f32[384]{0:T(512)} %param.9) | copy-start | bytes 4612
  31.7 4.5 copy-start.10
  31.7 33.1 %all-to-all-start = ((bf16[4,4,192,384]{3,2,1,0:T(8,128)(2,1)}), bf16[4,4,192,384]{3,2,1,0:T(8,128)(2,1)S(1)}, u32[]{:S(2)}, u32[]{:S(2)}) async-start(bf16[4,4,192,384]{3,2,1,0:T(8,128)(2,1)} %bitcast.69), calls=%async_computation | async-start | bytes 4718592 | tf_op jit(solution)/shard_map/all_to_all | solution.py:64
  64.7 1.5 copy-start.1
  66.2 33.0 %all-to-all-start.2 = ((bf16[4,4,192,384]{3,2,1,0:T(8,128)(2,1)}), bf16[4,4,192,384]{3,2,1,0:T(8,128)(2,1)}, u32[]{:S(2)}, u32[]{:S(2)}) async-start(bf16[4,4,192,384]{3,2,1,0:T(8,128)(2,1)} %bitcast.68), calls=%async_computation.2 | async-start | bytes 4718592 | tf_op jit(solution)/shard_map/all_to_all | solution.py:64
  70.7 290.6 %reduce-scatter.4.cloned.1.call-start = ((), (), s32[]{:S(2)}) async-start(), calls=%async_computation.9 | async-start | bytes 3538944 | tf_op jit(solution)/shard_map/reduce_scatter | solution.py:102
  228.2 150.4 %reduce-scatter.6.cloned.1.call-start = ((), (), s32[]{:S(2)}) async-start(), calls=%async_computation.10 | async-start | bytes 3538944 | tf_op jit(solution)/shard_map/reduce_scatter | solution.py:105
  235.8 1.7 copy-start.7
  235.9 220.0 %reduce-scatter.8.cloned.1.call-start = ((), (), s32[]{:S(2)}) async-start(), calls=%async_computation.11 | async-start | bytes 3538944 | tf_op jit(solution)/shard_map/reduce_scatter | solution.py:108
  245.5 6.7 %slice-start = ((s8[6291456]{0:T(1024)(128)(4,1)}), s8[2097152]{0:T(1024)(128)(4,1)S(1)}, s32[]{:S(2)}) async-start(s8[6291456]{0:T(1024)(128)(4,1)} %bitcast.81), calls=%async_computation.13 | async-start | bytes 4194304
  245.5 6.7 %copy-start.6 = (bf16[4,384,1024]{2,1,0:T(8,128)(2,1)S(1)}, bf16[4,384,1024]{2,1,0:T(8,128)(2,1)}, u32[]{:S(2)}) copy-start(bf16[4,384,1024]{2,1,0:T(8,128)(2,1)} %all-gather.7.cloned.1.call-done) | copy-start | bytes 9437188
  245.5 6.8 %slice-start.1 = ((s8[6291456]{0:T(1024)(128)(4,1)}), s8[4194304]{0:T(1024)(128)(4,1)S(1)}, s32[]{:S(2)}) async-start(s8[6291456]{0:T(1024)(128)(4,1)} %bitcast.81), calls=%async_computation.14 | async-start | bytes 8388608
  259.3 32.1 %all-to-all-start.3 = ((bf16[1,4,768,384]{3,1,0,2:T(4,128)(2,1)}), bf16[1,4,768,384]{3,1,0,2:T(4,128)(2,1)S(1)}, u32[]{:S(2)}, u32[]{:S(2)}) async-start(bf16[1,4,768,384]{3,1,0,2:T(4,128)(2,1)} %copy.44), calls=%async_computation.3 | async-start | bytes 4718592 | tf_op jit(solution)/shard_map/all_to_all | solution.py:68
  291.4 1.4 copy-start.2
  292.8 33.2 %all-to-all-start.1 = ((bf16[1,4,768,384]{3,1,0,2:T(4,128)(2,1)}), bf16[1,4,768,384]{3,1,0,2:T(4,128)(2,1)}, u32[]{:S(2)}, u32[]{:S(2)}) async-start(bf16[1,4,768,384]{3,1,0,2:T(4,128)(2,1)} %copy.40), calls=%async_computation.1 | async-start | bytes 4718592 | tf_op jit(solution)/shard_map/all_to_all | solution.py:68
  297.4 2.6 copy-start.3
  337.2 5.0 %copy-start.4 = (f32[1024,384]{1,0:T(8,128)S(1)}, f32[1024,384]{1,0:T(8,128)}, u32[]{:S(2)}) copy-start(f32[1024,384]{1,0:T(8,128)} %convert_element_type.81) | copy-start | bytes 4718596
  337.2 5.0 %copy-start.5 = (f32[1024,2]{1,0:T(8,128)S(1)}, f32[1024,2]{1,0:T(8,128)}, u32[]{:S(2)}) copy-start(f32[1024,2]{1,0:T(8,128)} %copy.34) | copy-start | bytes 24580
Sparse Core Ops, SparseCore 0:
  10.2 62.7 all-gather.8
  75.2 58.6 all-gather.4
  136.1 58.6 all-gather.6
  228.3 73.2 reduce-scatter.3
  305.1 73.4 reduce-scatter.5
  382.0 73.8 reduce-scatter.7
